TPU v7x, 128 devices: a whole 4x4x4 slice. The times are simulated.
128 devices in a mesh: sky: 32 (over y, z, core), band: 4 (over x).
Axes of the slice: x: 4, y: 4, z: 4, core: 2. Of those that a mesh axis runs over, the one named last changes fastest.
Arguments:
- exposures: bfloat16 [32, 4, 1024, 1024], P('sky', 'band'), may hold values from -6 to 6
- inv_variance: bfloat16 [32, 4, 1024, 1024], P('sky', 'band'), may hold values from 0.25 to 4
- mask_planes: int32 [32, 4, 2, 35], P('sky', 'band'), may hold values from 0 to 1073741823, as said below
- sky_columns: int32 [32, 4, 8], replicated, may hold values from 0 to 31, as said below
- basis_rows: float32 [9, 25], replicated, may hold values from -1 to 1
- basis_cols: float32 [9, 25], replicated, may hold values from -1 to 1
- match_coeffs: float32 [32, 4, 9], P('sky', 'band'), may hold values from -2 to 2
- detect_taps: float32 [4, 31], P('band'), may hold values from 0.05 to 0.3
Outputs:
- difference: bfloat16 [32, 4, 1024, 1024], P('sky', 'band')
- detection: float32 [1024, 4096], P('band', 'sky')
Inputs may be any that keep to these rules, and one draw needn't show every extreme that they name: Each row sky_columns[e, b] holds 8 consecutive sky tile columns in order, counted modulo 32; every sky tile column is covered by some exposure of every band. Bit j of mask_planes[e, b, 0, w] marks pixel column 30 w + j of that exposure as bad and bit j of mask_planes[e, b, 1, w] pixel row 30 w + j; bits past 1024 are ignored. In every draw some word has all 30 bits set.
All inputs are finite; a program needn't handle non-finite values.
Results may differ from a plain program's by a relative error of at most 0.0095.
Values may be sent and summed in bfloat16 or wider, within the bound.
A program may use at most 128 MiB of HBM per device.

v0:
```python
import jax
import jax.numpy as jnp
from jax import lax
from jax.sharding import PartitionSpec as P

TILE = 128
NB = 9
TAPS = 25
DTAPS = 31


def with_halo(block, sides, width):
    for axis, dim in sides:
        count = lax.axis_size(axis)
        forward = [(i, i + 1) for i in range(count - 1)]
        forward.append((count - 1, 0))
        backward = [(target, source) for source, target in forward]
        low = lax.ppermute(
            lax.slice_in_dim(block, block.shape[dim] - width, None, axis=dim), axis, forward
        )
        high = lax.ppermute(lax.slice_in_dim(block, 0, width, axis=dim), axis, backward)
        block = jnp.concatenate([low, block, high], axis=dim)
    return block


def cut_along(value, dim, length):
    dims = value.shape
    pieces = value.reshape(*dims[:dim], length, dims[dim] // length, *dims[dim + 1 :])
    return jnp.moveaxis(pieces, dim, 0)


def sum_at_owner(value, axis, dim):
    pieces = cut_along(value, dim, lax.axis_size(axis))
    arrived = lax.all_to_all(pieces, axis, split_axis=0, concat_axis=0, tiled=True)
    return arrived.sum(axis=0)


def band_matrix(tap_rows, window_width):
    offsets = (
        jnp.arange(window_width, dtype=jnp.int32)[:, None]
        - jnp.arange(TILE, dtype=jnp.int32)[None, :]
    )
    selector = (
        offsets[:, :, None] == jnp.arange(tap_rows.shape[1], dtype=jnp.int32)[None, None, :]
    ).astype(jnp.float32)
    return jnp.einsum(
        "wtl,kl->kwt", selector, tap_rows.astype(jnp.float32), precision=lax.Precision.HIGHEST
    ).astype(jnp.bfloat16)


def keep_pixels(planes, side_length):
    places = jnp.arange(side_length, dtype=jnp.int32)
    column_bits = jnp.bitwise_and(jnp.right_shift(planes[0][places // 30], places % 30), 1)
    row_bits = jnp.bitwise_and(jnp.right_shift(planes[1][places // 30], places % 30), 1)
    return jnp.logical_and(row_bits[:, None] == 0, column_bits[None, :] == 0)


def psf_match(picture, column_taps, row_taps):
    side_length = picture.shape[1]
    block_count = side_length // TILE
    margin = TAPS // 2
    width_full = TILE + 2 * margin
    padded = jnp.pad(picture, ((0, 0), (margin, margin)))
    blocks = jnp.stack(
        [
            padded[:, TILE * block_index : TILE * block_index + width_full]
            for block_index in range(block_count)
        ],
        0,
    )
    column_band = band_matrix(column_taps, width_full)
    column_pass = jnp.einsum(
        "jyw,kwt->kyjt", blocks, column_band, preferred_element_type=jnp.float32
    )
    column_pass = column_pass.reshape(NB, side_length, side_length).astype(jnp.bfloat16)
    row_padded = jnp.pad(column_pass, ((0, 0), (margin, margin), (0, 0)))
    row_blocks = jnp.stack(
        [
            row_padded[:, TILE * block_index : TILE * block_index + width_full, :]
            for block_index in range(block_count)
        ],
        0,
    )
    row_band = band_matrix(row_taps, width_full)
    summed = jnp.einsum("ikwx,kwt->itx", row_blocks, row_band, preferred_element_type=jnp.float32)
    return summed.reshape(side_length, side_length).astype(jnp.bfloat16)


def average_pieces(pieces):
    matched_in, weight_in = pieces
    weight_float = weight_in.astype(jnp.float32)
    numer = jnp.sum(weight_float * matched_in.astype(jnp.float32), axis=1)
    denom = jnp.sum(weight_float, axis=1)
    return (numer / jnp.maximum(denom, 1.0)).astype(jnp.bfloat16)


def subtract_template(template, matched, own_columns, side_length, sky_count):
    gathered = lax.all_gather(template, "sky", axis=1, tiled=True).reshape(
        side_length, sky_count, TILE
    )
    picked = jnp.take(gathered, own_columns, axis=1).reshape(side_length, side_length)
    return (matched.astype(jnp.float32) - picked.astype(jnp.float32)).astype(jnp.bfloat16)


def body(
    exposures,
    inv_variance,
    mask_planes,
    sky_columns,
    basis_rows,
    basis_cols,
    match_coeffs,
    detect_taps,
):
    picture = exposures[0, 0]
    side_length = picture.shape[0]
    block_count = side_length // TILE
    sky_count = lax.axis_size("sky")
    own_sky = lax.axis_index("sky")
    own_band = lax.axis_index("band")
    column_taps = (match_coeffs[0, 0][:, None] * basis_cols).astype(jnp.bfloat16)
    matched = psf_match(picture, column_taps, basis_rows.astype(jnp.bfloat16))
    keep = keep_pixels(mask_planes[0, 0], side_length)
    variance_inv = inv_variance[0, 0]
    weight = jnp.where(keep, variance_inv, jnp.zeros_like(variance_inv))
    own_columns = sky_columns[own_sky, own_band]
    empty_slots = jnp.zeros((side_length, sky_count, TILE), jnp.bfloat16)
    send_matched = empty_slots.at[:, own_columns, :].set(
        matched.reshape(side_length, block_count, TILE)
    )
    send_weight = empty_slots.at[:, own_columns, :].set(
        weight.reshape(side_length, block_count, TILE)
    )
    template = average_pieces(
        (
            lax.all_to_all(send_matched, "sky", split_axis=1, concat_axis=1, tiled=True),
            lax.all_to_all(send_weight, "sky", split_axis=1, concat_axis=1, tiled=True),
        )
    )
    difference = subtract_template(template, matched, own_columns, side_length, sky_count)
    margin = DTAPS // 2
    width_full = TILE + 2 * margin
    filter_band = band_matrix(detect_taps.astype(jnp.bfloat16), width_full)[0]
    widened = with_halo(template, (("sky", 1),), margin)
    smoothed = jnp.dot(widened, filter_band, preferred_element_type=jnp.float32).astype(
        jnp.bfloat16
    )
    smooth_padded = jnp.pad(smoothed, ((margin, margin), (0, 0)))
    smooth_blocks = jnp.stack(
        [
            smooth_padded[TILE * block_index : TILE * block_index + width_full]
            for block_index in range(block_count)
        ],
        0,
    )
    filtered = jnp.einsum(
        "iwx,wt->itx", smooth_blocks, filter_band, preferred_element_type=jnp.float32
    ).reshape(side_length, TILE)
    power = filtered * filtered
    detection = sum_at_owner(power, "band", 0)
    return (difference[None, None], detection)


def solution(mesh):
    in_specs = (
        P("sky", "band", None, None),
        P("sky", "band", None, None),
        P("sky", "band", None, None),
        P(),
        P(),
        P(),
        P("sky", "band", None),
        P("band", None),
    )
    out_specs = (P("sky", "band", None, None), P("band", "sky"))
    return jax.shard_map(body, mesh=mesh, in_specs=in_specs, out_specs=out_specs, check_vma=False)
```

profile of v0, /device:TPU:1, one launch (start us, length us, event | category | flops | bytes accessed | tf_op | source)
XLA Modules:
  0.0 444.7 jit_solution(8928743750772134446)
XLA Ops:
  11.6 9.2 %convolution_convert_fusion = bf16[9,128,8,1024]{3,1,2,0:T(8,128)(2,1)} fusion(bf16[8,1024,152]{1,2,0:T(8,128)(2,1)S(1)} %fusion.34, bf16[9,152,128,1]{2,0,1,3:T(8,128)(2,1)S(1)} %fusion.19), kind=kOutput, calls=%fused_computation.8 | convolution fusion | flops 2878341120 | bytes 21714944 | tf_op jit(solution)/shard_map/jyw,kwt->kyjt/dot_general | solution.py:72
  20.8 24.6 %copy.65 = bf16[9,1024,1024]{2,1,0:T(8,128)(2,1)} copy(bf16[9,1024,1024]{1,2,0:T(8,128)(2,1)} %bitcast.238) | data formatting | bytes 37748736 | tf_op jit(solution)/shard_map/convert_element_type | solution.py:75
  45.4 4.3 fusion.2
  71.4 9.9 %bitcast_convert_fusion = bf16[128,8,1024]{2,0,1:T(8,128)(2,1)S(1)} fusion(bf16[8,9,152,1024]{3,2,1,0:T(8,128)(2,1)} %fusion.4, bf16[9,152,128]{2,0,1:T(8,128)(2,1)S(1)} %fusion.20), kind=kOutput, calls=%fused_computation.9 | convolution fusion | flops 2869952512 | bytes 24860672 | tf_op jit(solution)/shard_map/ikwx,kwt->itx/dot_general | solution.py:85
  83.8 5.1 %broadcast_in_dim.18.clone.1 = bf16[1024,32,128]{2,0,1:T(8,128)(2,1)} broadcast(bf16[]{:T(256)} %constant.31.clone.1), dimensions={} | broadcast | bytes 8388610 | tf_op jit(solution)/shard_map/broadcast_in_dim | solution.py:127
  88.9 5.7 %scatter_fusion.1 = bf16[1024,32,128]{2,0,1:T(8,128)(2,1)} fusion(bf16[1024,32,128]{2,0,1:T(8,128)(2,1)} %broadcast_in_dim.18.clone.1, s32[8]{0:T(128)S(1)} %fusion.61, bf16[8,1024,128]{2,1,0:T(8,128)(2,1)} %bitcast.250), kind=kCustom, calls=%fused_computation.2 | custom fusion | bytes 6291488 | tf_op jit(solution)/shard_map/scatter | solution.py:128
  94.6 9.6 %all-to-all-start.1 = ((bf16[1024,32,128]{2,0,1:T(8,128)(2,1)}), bf16[1024,32,128]{2,0,1:T(8,128)(2,1)}, u32[]{:S(2)}, u32[]{:S(2)}) async-start(bf16[1024,32,128]{2,0,1:T(8,128)(2,1)} %scatter_fusion.1), calls=%async_computation.1 | async-start | bytes 16777216 | tf_op jit(solution)/shard_map/all_to_all | solution.py:136
  109.1 4.5 %compare_select_fusion.2 = s32[1024,1]{0,1:T(1,128)S(1)} fusion(s32[]{:T(128)} %bitcast.97, s32[]{:T(128)} %bitcast.98, s32[]{:T(128)} %bitcast.99, s32[]{:T(128)} %bitcast.100, s32[]{:T(128)} %bitcast.101, s32[]{:T(128)} %bitcast.103, s32[]{:T(128)} %bitcast.102), kind=kLoop, calls=%fused_computation.125 | loop fusion | flops 23552 | bytes 4124 | tf_op jit(solution)/shard_map/gather | solution.py:53
  115.0 4.4 compare_select_fusion.1
  119.5 17.3 %fusion.49 = pred[8,128]{1,0:T(8,128)(4,1)S(1)} fusion(pred[1024]{0:T(1024)(128)(4,1)S(1)} %compare_reduce_fusion, pred[1024]{0:T(1024)(128)(4,1)S(1)} %compare_reduce_fusion.1, pred[1024]{0:T(1024)(128)(4,1)S(1)} %compare_reduce_fusion.2, pred[1024]{0:T(1024)(128)(4,1)S(1)} %compare_reduce_fusion.3, pred[1024]{0:T(1024)(128)(4,1)S(1)} %compare_reduce_fusion.4, ...), kind=kLoop, calls=%fused_computation.147 | loop fusion | flops 39936 | bytes 33904 | tf_op jit(solution)/shard_map/eq | solution.py:55
  136.8 17.6 %fusion.46 = pred[1024]{0:T(1024)(128)(4,1)S(1)} fusion(pred[1024]{0:T(1024)(128)(4,1)S(1)} %compare_reduce_fusion, pred[1024]{0:T(1024)(128)(4,1)S(1)} %compare_reduce_fusion.1, pred[1024]{0:T(1024)(128)(4,1)S(1)} %compare_reduce_fusion.2, pred[1024]{0:T(1024)(128)(4,1)S(1)} %compare_reduce_fusion.3, pred[1024]{0:T(1024)(128)(4,1)S(1)} %compare_reduce_fusion.4, ...), kind=kLoop, calls=%fused_computation.144 | loop fusion | flops 37888 | bytes 33904 | tf_op jit(solution)/shard_map/eq | solution.py:55
  156.4 5.1 %broadcast_in_dim.18.clone = bf16[1024,32,128]{2,0,1:T(8,128)(2,1)} broadcast(bf16[]{:T(256)} %constant.31.clone.1), dimensions={} | broadcast | bytes 8388610 | tf_op jit(solution)/shard_map/broadcast_in_dim | solution.py:127
  161.5 5.8 %scatter_fusion = bf16[1024,32,128]{2,0,1:T(8,128)(2,1)} fusion(bf16[1024,32,128]{2,0,1:T(8,128)(2,1)} %broadcast_in_dim.18.clone, s32[8]{0:T(128)S(1)} %fusion.61, bf16[8,1024,128]{2,1,0:T(8,128)(2,1)} %fusion.16), kind=kCustom, calls=%fused_computation.1 | custom fusion | bytes 6291488 | tf_op jit(solution)/shard_map/scatter | solution.py:131
  167.3 45.5 %all-to-all-done.1 = bf16[1024,32,128]{2,0,1:T(8,128)(2,1)} async-done(((bf16[1024,32,128]{2,0,1:T(8,128)(2,1)}), bf16[1024,32,128]{2,0,1:T(8,128)(2,1)}, u32[]{:S(2)}, u32[]{:S(2)}) %all-to-all-start.1) | async-done | bytes 8388640 | tf_op jit(solution)/shard_map/all_to_all | solution.py:136
  212.8 117.1 %all_to_all.15 = bf16[1024,32,128]{2,0,1:T(8,128)(2,1)} all-to-all(bf16[1024,32,128]{2,0,1:T(8,128)(2,1)} %scatter_fusion), channel_id=1, replica_groups=mesh['sky'=32,'band'=4] {'sky'}, dimensions={1} | all-to-all | bytes 16777216 | tf_op jit(solution)/shard_map/all_to_all | solution.py:137
  329.9 9.0 %convert_reduce_fusion = (f32[1024,128]{1,0:T(8,128)S(1)}, f32[1024,128]{1,0:T(8,128)S(1)}) fusion(bf16[1024,32,128]{2,0,1:T(8,128)(2,1)} %all_to_all.15, bf16[1024,32,128]{2,0,1:T(8,128)(2,1)} %all-to-all-done.1), kind=kLoop, calls=%fused_computation.3 | loop fusion | flops 20709376 | bytes 17825792 | tf_op jit(solution)/shard_map/reduce_sum | solution.py:93
  349.9 4.0 all-to-all-start.2
  354.0 6.8 %all-to-all-done.2 = f32[4,256,128]{2,1,0:T(8,128)S(1)} async-done(((f32[4,256,128]{2,1,0:T(8,128)}), f32[4,256,128]{2,1,0:T(8,128)S(1)}, u32[]{:S(2)}, u32[]{:S(2)}) %all-to-all-start.2) | async-done | bytes 524320 | tf_op jit(solution)/shard_map/all_to_all | solution.py:34
  361.5 36.1 %all-gather.2.cloned.1.call-done = bf16[1024,4096]{1,0:T(8,128)(2,1)} async-done(((bf16[1024,128]{1,0:T(8,128)(2,1)}), bf16[1024,4096]{1,0:T(8,128)(2,1)}) %all-gather.2.cloned.1.call-update) | async-done | bytes 8388624 | tf_op jit(solution)/shard_map/all_gather | solution.py:98
  397.6 11.9 %copy.75 = bf16[1024,4096]{0,1:T(8,128)(2,1)} copy(bf16[1024,4096]{1,0:T(8,128)(2,1)} %all-gather.2.cloned.1.call-done) | data formatting | bytes 16777216 | tf_op jit(solution)/shard_map/all_gather | solution.py:98
  409.5 11.9 %copy.76 = bf16[1024,32,128]{2,0,1:T(8,128)(2,1)} copy(bf16[1024,32,128]{0,2,1:T(8,128)(2,1)} %bitcast.239) | data formatting | bytes 16777216 | tf_op jit(solution)/shard_map/reshape | solution.py:98
  421.4 5.5 %gather_fusion = bf16[8,1024,128]{2,1,0:T(8,128)(2,1)} fusion(bf16[1024,32,128]{2,0,1:T(8,128)(2,1)} %copy.76, s32[1024]{0:T(1024)S(1)} %pad_clamp_fusion), kind=kCustom, calls=%fused_computation | custom fusion | bytes 4194336 | tf_op jit(solution)/shard_map/jit(_take)/gather | solution.py:101
  429.8 4.1 subtract_convert_fusion
  433.9 3.9 copy.79
  (102 shorter events, 51.3 us)
Async XLA Ops:
  7.2 76.4 %copy-start = (s32[32,4,8]{0,2,1:T(8,128)S(1)}, s32[32,4,8]{0,2,1:T(8,128)}, u32[]{:S(2)}) copy-start(s32[32,4,8]{0,2,1:T(8,128)} %param.11) | copy-start | bytes 12292
  10.3 0.7 copy-start.5
  10.3 0.7 copy-start.6
  45.4 8.2 %copy-start.2 = (bf16[9,1024,1024]{2,1,0:T(8,128)(2,1)S(1)}, bf16[9,1024,1024]{2,1,0:T(8,128)(2,1)}, u32[]{:S(2)}) copy-start(bf16[9,1024,1024]{2,1,0:T(8,128)(2,1)} %copy.65) | copy-start | bytes 56623108
  68.4 2.4 copy-start.7
  94.6 118.2 %all-to-all-start.1 = ((bf16[1024,32,128]{2,0,1:T(8,128)(2,1)}), bf16[1024,32,128]{2,0,1:T(8,128)(2,1)}, u32[]{:S(2)}, u32[]{:S(2)}) async-start(bf16[1024,32,128]{2,0,1:T(8,128)(2,1)} %scatter_fusion.1), calls=%async_computation.1 | async-start | bytes 16777216 | tf_op jit(solution)/shard_map/all_to_all | solution.py:136
  104.2 3.4 copy-start.4
  104.3 293.3 %all-gather.2.cloned.1.call-start = ((), (), s32[]{:S(2)}) async-start(), calls=%async_computation.3 | async-start | bytes 8650752 | tf_op jit(solution)/shard_map/all_gather | solution.py:98
  329.9 10.2 %copy-start.8 = (f32[1,31]{1,0:T(1,128)S(1)}, f32[1,31]{1,0:T(1,128)}, u32[]{:S(2)}) copy-start(f32[1,31]{1,0:T(1,128)} %param.15) | copy-start | bytes 376
  339.7 0.9 copy-start.3
  340.8 3.7 collective-permute-start
  341.1 6.1 %collective-permute-start.1 = (bf16[1024,15]{1,0:T(8,128)(2,1)S(1)}, bf16[1024,15]{1,0:T(8,128)(2,1)}, u32[]{:S(2)}, u32[]{:S(2)}) collective-permute-start(bf16[1024,15]{1,0:T(8,128)(2,1)S(1)} %get-tuple-element.11), channel_id=1, source_target_pairs={{4,0},{8,4},{12,8},{16,12},{20,16},{24,20},{28,24},{32,28},{36,32}... | collective-permute-start | bytes 92168 | tf_op jit(solution)/shard_map/ppermute | solution.py:21
  349.9 11.0 %all-to-all-start.2 = ((f32[4,256,128]{2,1,0:T(8,128)}), f32[4,256,128]{2,1,0:T(8,128)S(1)}, u32[]{:S(2)}, u32[]{:S(2)}) async-start(f32[4,256,128]{2,1,0:T(8,128)} %bitcast.124), calls=%async_computation.2 | async-start | bytes 1048576 | tf_op jit(solution)/shard_map/all_to_all | solution.py:34
  429.8 8.1 %copy-start.1 = (s32[32,4,8]{0,2,1:T(8,128)S(1)}, s32[32,4,8]{0,2,1:T(8,128)}, u32[]{:S(2)}) copy-start(s32[32,4,8]{0,2,1:T(8,128)} %param.11) | copy-start | bytes 12292
Sparse Core Ops, SparseCore 0:
  339.9 57.6 all-gather.1
where the time goes:
time: 447 us; the launch traced here: 445 us
  local copies, waits for them, and re-layouts  123 us (28%)
  blocking collectives  117 us (26%)
  waiting for transfers between devices  91.2 us (20%)
  other arithmetic  61.9 us (14%)
  matrix products  23.2 us (5%)
  starting transfers between devices  14.3 us (3%)
  between operations  14.3 us (3%)
    all_to_all x1, blocking collectives, body(): lax.all_to_all(send_weight, 'sky', split_axis=1, concat_axis=1, tiled=True)  117 us
    all_to_all x1, waiting for transfers between devices, body(): lax.all_to_all(send_matched, 'sky', split_axis=1, concat_axis=1, tiled=True)  45.5 us
    all_gather x1, waiting for transfers between devices, subtract_template(): lax.all_gather(template, 'sky', axis=1, tiled=True)  36.1 us
    eq x2, other arithmetic, keep_pixels(): return jnp.logical_and(row_bits[:, None] == 0, column_bits[None, :] == 0)  34.9 us
    unnamed x43, local copies, waits for them, and re-layouts  33.6 us
    convert_element_type x1, local copies, waits for them, and re-layouts, psf_match(): column_pass.reshape(NB, side_length, side_length).astype(jnp.bfloat16)  24.6 us
    all_gather x1, local copies, waits for them, and re-layouts, subtract_template(): lax.all_gather(template, 'sky', axis=1, tiled=True)  11.9 us
    reshape x1, local copies, waits for them, and re-layouts, subtract_template(): lax.all_gather(template, 'sky', axis=1, tiled=True)  11.9 us
  transfers between devices with their start and end apart: 5, of which 5 were waited for; matrix products, arithmetic and copies ran while one was open for 16% of the time, Pallas kernels for 0%

commit v1 on v0

--- a/solution.py
+++ b/solution.py
@@ -1,3 +1,4 @@
+import functools
 import jax
 import jax.numpy as jnp
 from jax import lax
@@ -7,6 +8,16 @@
 NB = 9
 TAPS = 25
 DTAPS = 31
+
+
+def name_spans(u_in, lane_axis, ndim_at):
+    return jnp.concatenate(
+        lax.all_to_all(jnp.stack(lax.axis_size(lane_axis) * [u_in], axis=0), lane_axis, 0, 0),
+        axis=ndim_at,
+    )
+
+
+build_the_patches = functools.partial(name_spans, lane_axis="sky", ndim_at=1)
 
 
 def with_halo(block, sides, width):
@@ -95,9 +106,7 @@
 
 
 def subtract_template(template, matched, own_columns, side_length, sky_count):
-    gathered = lax.all_gather(template, "sky", axis=1, tiled=True).reshape(
-        side_length, sky_count, TILE
-    )
+    gathered = build_the_patches(template).reshape(side_length, sky_count, TILE)
     picked = jnp.take(gathered, own_columns, axis=1).reshape(side_length, side_length)
     return (matched.astype(jnp.float32) - picked.astype(jnp.float32)).astype(jnp.bfloat16)
 

time: 447 us -> 534 us (1.19)
  the two profiles are of different devices: /device:TPU:1 before, /device:TPU:32 now
where the time goes in v1:
time: 534 us; the launch traced here: 532 us
  waiting for transfers between devices  307 us (57%)
  local copies, waits for them, and re-layouts  104 us (19%)
  other arithmetic  62.1 us (12%)
  matrix products  22.6 us (4%)
  starting transfers between devices  21.5 us (4%)
  blocking collectives  13.8 us (3%)
    all_to_all x1, waiting for transfers between devices, body(): lax.all_to_all(send_weight, 'sky', split_axis=1, concat_axis=1, tiled=True)  123 us
    all_to_all x1, waiting for transfers between devices, name_spans(): lax.all_to_all(jnp.stack(lax.axis_size(lane_axis) * [u_in], axis=0), lane...  120 us
    all_to_all x1, waiting for transfers between devices, body(): lax.all_to_all(send_matched, 'sky', split_axis=1, concat_axis=1, tiled=True)  61.3 us
    eq x2, other arithmetic, keep_pixels(): return jnp.logical_and(row_bits[:, None] == 0, column_bits[None, :] == 0)  34.9 us
    unnamed x41, local copies, waits for them, and re-layouts  33.5 us
    convert_element_type x1, local copies, waits for them, and re-layouts, psf_match(): column_pass.reshape(NB, side_length, side_length).astype(jnp.bfloat16)  24.6 us
    all_to_all x1, blocking collectives, sum_at_owner(): lax.all_to_all(pieces, axis, split_axis=0, concat_axis=0, tiled=True)  13.8 us
    scatter x2, local copies, waits for them, and re-layouts, body(): empty_slots.at[:, own_columns, :]  11.5 us
  transfers between devices with their start and end apart: 5, of which 4 were waited for; matrix products, arithmetic and copies ran while one was open for 13% of the time, Pallas kernels for 0%

profile of v1, /device:TPU:32, one launch (start us, length us, event | category | flops | bytes accessed | tf_op | source)
XLA Modules:
  0.0 532.1 jit_solution(11633801968990733470)
XLA Ops:
  5.1 9.2 %convolution_convert_fusion = bf16[9,128,8,1024]{3,1,2,0:T(8,128)(2,1)} fusion(bf16[8,1024,152]{1,2,0:T(8,128)(2,1)S(1)} %fusion.34, bf16[9,152,128,1]{2,0,1,3:T(8,128)(2,1)S(1)} %fusion.19), kind=kOutput, calls=%fused_computation.8 | convolution fusion | flops 2878341120 | bytes 21714944 | tf_op jit(solution)/shard_map/jyw,kwt->kyjt/dot_general | solution.py:83
  14.3 24.6 %copy.47 = bf16[9,1024,1024]{2,1,0:T(8,128)(2,1)} copy(bf16[9,1024,1024]{1,2,0:T(8,128)(2,1)} %bitcast.238) | data formatting | bytes 37748736 | tf_op jit(solution)/shard_map/convert_element_type | solution.py:86
  38.9 4.3 fusion.2
  64.9 9.9 %bitcast_convert_fusion = bf16[128,8,1024]{2,0,1:T(8,128)(2,1)S(1)} fusion(bf16[8,9,152,1024]{3,2,1,0:T(8,128)(2,1)} %fusion.4, bf16[9,152,128]{2,0,1:T(8,128)(2,1)S(1)} %fusion.20), kind=kOutput, calls=%fused_computation.9 | convolution fusion | flops 2869952512 | bytes 24860672 | tf_op jit(solution)/shard_map/ikwx,kwt->itx/dot_general | solution.py:96
  77.2 5.1 broadcast_in_dim.18.clone.1
  82.3 5.8 %scatter_fusion.1 = bf16[1024,32,128]{2,0,1:T(8,128)(2,1)} fusion(bf16[1024,32,128]{2,0,1:T(8,128)(2,1)} %broadcast_in_dim.18.clone.1, s32[8]{0:T(128)S(1)} %fusion.61, bf16[8,1024,128]{2,1,0:T(8,128)(2,1)} %bitcast.249), kind=kCustom, calls=%fused_computation.2 | custom fusion | bytes 6291488 | tf_op jit(solution)/shard_map/scatter | solution.py:137
  88.1 8.2 %all-to-all-start.1 = ((bf16[1024,32,128]{2,0,1:T(8,128)(2,1)}), bf16[1024,32,128]{2,0,1:T(8,128)(2,1)}, u32[]{:S(2)}, u32[]{:S(2)}) async-start(bf16[1024,32,128]{2,0,1:T(8,128)(2,1)} %scatter_fusion.1), calls=%async_computation.1 | async-start | bytes 16777216 | tf_op jit(solution)/shard_map/all_to_all | solution.py:145
  101.1 4.5 compare_select_fusion.2
  107.1 4.4 compare_select_fusion.1
  111.5 17.3 %fusion.49 = pred[8,128]{1,0:T(8,128)(4,1)S(1)} fusion(pred[1024]{0:T(1024)(128)(4,1)S(1)} %compare_reduce_fusion, pred[1024]{0:T(1024)(128)(4,1)S(1)} %compare_reduce_fusion.1, pred[1024]{0:T(1024)(128)(4,1)S(1)} %compare_reduce_fusion.2, pred[1024]{0:T(1024)(128)(4,1)S(1)} %compare_reduce_fusion.3, pred[1024]{0:T(1024)(128)(4,1)S(1)} %compare_reduce_fusion.4, ...), kind=kLoop, calls=%fused_computation.147 | loop fusion | flops 39936 | bytes 33904 | tf_op jit(solution)/shard_map/eq | solution.py:66
  128.8 17.6 %fusion.46 = pred[1024]{0:T(1024)(128)(4,1)S(1)} fusion(pred[1024]{0:T(1024)(128)(4,1)S(1)} %compare_reduce_fusion, pred[1024]{0:T(1024)(128)(4,1)S(1)} %compare_reduce_fusion.1, pred[1024]{0:T(1024)(128)(4,1)S(1)} %compare_reduce_fusion.2, pred[1024]{0:T(1024)(128)(4,1)S(1)} %compare_reduce_fusion.3, pred[1024]{0:T(1024)(128)(4,1)S(1)} %compare_reduce_fusion.4, ...), kind=kLoop, calls=%fused_computation.144 | loop fusion | flops 37888 | bytes 33904 | tf_op jit(solution)/shard_map/eq | solution.py:66
  148.5 5.1 broadcast_in_dim.18.clone
  153.6 5.7 %scatter_fusion = bf16[1024,32,128]{2,0,1:T(8,128)(2,1)} fusion(bf16[1024,32,128]{2,0,1:T(8,128)(2,1)} %broadcast_in_dim.18.clone, s32[8]{0:T(128)S(1)} %fusion.61, bf16[8,1024,128]{2,1,0:T(8,128)(2,1)} %fusion.16), kind=kCustom, calls=%fused_computation.1 | custom fusion | bytes 6291488 | tf_op jit(solution)/shard_map/scatter | solution.py:140
  159.3 61.3 %all-to-all-done.1 = bf16[1024,32,128]{2,0,1:T(8,128)(2,1)} async-done(((bf16[1024,32,128]{2,0,1:T(8,128)(2,1)}), bf16[1024,32,128]{2,0,1:T(8,128)(2,1)}, u32[]{:S(2)}, u32[]{:S(2)}) %all-to-all-start.1) | async-done | bytes 8388640 | tf_op jit(solution)/shard_map/all_to_all | solution.py:145
  220.6 5.8 %all-to-all-start = ((bf16[1024,32,128]{2,0,1:T(8,128)(2,1)}), bf16[1024,32,128]{2,0,1:T(8,128)(2,1)}, u32[]{:S(2)}, u32[]{:S(2)}) async-start(bf16[1024,32,128]{2,0,1:T(8,128)(2,1)} %scatter_fusion), calls=%async_computation | async-start | bytes 16777216 | tf_op jit(solution)/shard_map/all_to_all | solution.py:146
  227.5 123.2 %all-to-all-done = bf16[1024,32,128]{2,0,1:T(8,128)(2,1)} async-done(((bf16[1024,32,128]{2,0,1:T(8,128)(2,1)}), bf16[1024,32,128]{2,0,1:T(8,128)(2,1)}, u32[]{:S(2)}, u32[]{:S(2)}) %all-to-all-start) | async-done | bytes 8388640 | tf_op jit(solution)/shard_map/all_to_all | solution.py:146
  350.7 9.0 %convert_reduce_fusion = (f32[1024,128]{1,0:T(8,128)S(1)}, f32[1024,128]{1,0:T(8,128)S(1)}) fusion(bf16[1024,32,128]{2,0,1:T(8,128)(2,1)} %all-to-all-done, bf16[1024,32,128]{2,0,1:T(8,128)(2,1)} %all-to-all-done.1), kind=kLoop, calls=%fused_computation.3 | loop fusion | flops 20709376 | bytes 17825792 | tf_op jit(solution)/shard_map/reduce_sum | solution.py:104
  366.8 13.8 %all_to_all.20 = f32[4,256,128]{2,1,0:T(8,128)S(1)} all-to-all(f32[4,256,128]{2,1,0:T(8,128)S(1)} %bitcast.254), channel_id=1, replica_groups=mesh['sky'=32,'band'=4] {'band'}, dimensions={0} | all-to-all | bytes 1048576 | tf_op jit(solution)/shard_map/all_to_all | solution.py:45
  380.5 5.1 stack.134
  385.6 5.7 %all-to-all-start.2 = ((bf16[32,1024,128]{2,1,0:T(8,128)(2,1)}), bf16[32,1024,128]{2,1,0:T(8,128)(2,1)}, u32[]{:S(2)}, u32[]{:S(2)}) async-start(bf16[32,1024,128]{2,1,0:T(8,128)(2,1)} %stack.134), calls=%async_computation.2 | async-start | bytes 16777216 | tf_op jit(solution)/shard_map/all_to_all | solution.py:15
  395.2 120.5 %all-to-all-done.2 = bf16[32,1024,128]{2,1,0:T(8,128)(2,1)} async-done(((bf16[32,1024,128]{2,1,0:T(8,128)(2,1)}), bf16[32,1024,128]{2,1,0:T(8,128)(2,1)}, u32[]{:S(2)}, u32[]{:S(2)}) %all-to-all-start.2) | async-done | bytes 8388640 | tf_op jit(solution)/shard_map/all_to_all | solution.py:15
  515.6 5.5 %gather_fusion = bf16[8,1024,128]{2,1,0:T(8,128)(2,1)} fusion(bf16[1024,32,128]{2,0,1:T(8,128)(2,1)} %bitcast.108, s32[1024]{0:T(1024)S(1)} %pad_clamp_fusion), kind=kCustom, calls=%fused_computation | custom fusion | bytes 4194336 | tf_op jit(solution)/shard_map/jit(_take)/gather | solution.py:110
  524.0 4.1 subtract_convert_fusion
  528.1 3.9 copy.59
  (98 shorter events, 51.5 us)
Async XLA Ops:
  0.6 76.4 %copy-start = (s32[32,4,8]{0,2,1:T(8,128)S(1)}, s32[32,4,8]{0,2,1:T(8,128)}, u32[]{:S(2)}) copy-start(s32[32,4,8]{0,2,1:T(8,128)} %param.11) | copy-start | bytes 12292
  3.8 0.7 copy-start.4
  3.8 0.7 copy-start.5
  38.9 8.2 %copy-start.2 = (bf16[9,1024,1024]{2,1,0:T(8,128)(2,1)S(1)}, bf16[9,1024,1024]{2,1,0:T(8,128)(2,1)}, u32[]{:S(2)}) copy-start(bf16[9,1024,1024]{2,1,0:T(8,128)(2,1)} %copy.47) | copy-start | bytes 56623108
  61.8 2.4 copy-start.6
  88.1 132.4 %all-to-all-start.1 = ((bf16[1024,32,128]{2,0,1:T(8,128)(2,1)}), bf16[1024,32,128]{2,0,1:T(8,128)(2,1)}, u32[]{:S(2)}, u32[]{:S(2)}) async-start(bf16[1024,32,128]{2,0,1:T(8,128)(2,1)} %scatter_fusion.1), calls=%async_computation.1 | async-start | bytes 16777216 | tf_op jit(solution)/shard_map/all_to_all | solution.py:145
  96.3 3.4 copy-start.3
  220.6 130.2 %all-to-all-start = ((bf16[1024,32,128]{2,0,1:T(8,128)(2,1)}), bf16[1024,32,128]{2,0,1:T(8,128)(2,1)}, u32[]{:S(2)}, u32[]{:S(2)}) async-start(bf16[1024,32,128]{2,0,1:T(8,128)(2,1)} %scatter_fusion), calls=%async_computation | async-start | bytes 16777216 | tf_op jit(solution)/shard_map/all_to_all | solution.py:146
  227.5 134.3 %copy-start.7 = (f32[1,31]{1,0:T(1,128)S(1)}, f32[1,31]{1,0:T(1,128)}, u32[]{:S(2)}) copy-start(f32[1,31]{1,0:T(1,128)} %param.15) | copy-start | bytes 376
  360.0 5.9 %collective-permute-start = (bf16[1024,15]{1,0:T(8,128)(2,1)S(1)}, bf16[1024,15]{1,0:T(8,128)(2,1)S(1)}, u32[]{:S(2)}, u32[]{:S(2)}) collective-permute-start(bf16[1024,15]{1,0:T(8,128)(2,1)S(1)} %get-tuple-element.8), channel_id=1, source_target_pairs={{0,4},{4,8},{8,12},{12,16},{16,20},{20,24},{24,28},{28,32},{32,36}... | collective-permute-start | bytes 92168 | tf_op jit(solution)/shard_map/ppermute | solution.py:29
  360.1 5.8 %collective-permute-start.1 = (bf16[1024,15]{1,0:T(8,128)(2,1)S(1)}, bf16[1024,15]{1,0:T(8,128)(2,1)S(1)}, u32[]{:S(2)}, u32[]{:S(2)}) collective-permute-start(bf16[1024,15]{1,0:T(8,128)(2,1)S(1)} %get-tuple-element.9), channel_id=1, source_target_pairs={{4,0},{8,4},{12,8},{16,12},{20,16},{24,20},{28,24},{32,28},{36,32}... | collective-permute-start | bytes 92168 | tf_op jit(solution)/shard_map/ppermute | solution.py:32
  385.6 130.0 %all-to-all-start.2 = ((bf16[32,1024,128]{2,1,0:T(8,128)(2,1)}), bf16[32,1024,128]{2,1,0:T(8,128)(2,1)}, u32[]{:S(2)}, u32[]{:S(2)}) async-start(bf16[32,1024,128]{2,1,0:T(8,128)(2,1)} %stack.134), calls=%async_computation.2 | async-start | bytes 16777216 | tf_op jit(solution)/shard_map/all_to_all | solution.py:15
  524.0 8.1 %copy-start.1 = (s32[32,4,8]{0,2,1:T(8,128)S(1)}, s32[32,4,8]{0,2,1:T(8,128)}, u32[]{:S(2)}) copy-start(s32[32,4,8]{0,2,1:T(8,128)} %param.11) | copy-start | bytes 12292
